TPU v7x, 512 devices: a whole 4x4x16 slice. The times are simulated.
512 devices in a mesh: freq: 64 (over z, x_hi, core), space: 8 (over x_lo, y).
Axes of the slice: x: 4 (x_hi: 2, x_lo: 2; x = x_hi * 2 + x_lo), y: 4, z: 16, core: 2. Of those that a mesh axis runs over, the one named last changes fastest.
Arguments:
- series: bfloat16 [2048, 131072], P('freq', 'space')
- starts: int32 [7], replicated, may hold values from 0 to 1536, as said below
- freqs: int32 [64], replicated, may hold values from 0 to 511, as said below
- alpha: int32 [1], replicated, may hold values from 1 to 63
Outputs:
- spectra: bfloat16 [64, 2, 7, 131072], P('freq', None, None, 'space')
- gram: float32 [64, 2, 63, 63], P('freq')
Inputs may be any that keep to these rules, and one draw needn't show every extreme that they name: `starts`: increasing; the first is 0, the last 1536; consecutive ones lie 512 / 4 to 384 apart. `freqs`: 64 distinct bins, 0 and 511 among them.
All inputs are finite; a program needn't handle non-finite values.
Results may differ from a plain program's by a relative error of at most 0.005.
Values may be sent and summed in bfloat16 or wider, within the bound.
No kernel may reach another device: no remote copies, remote signals or barrier semaphores. Data moves between devices by JAX's collectives and lax.ppermute only.
A program may use at most 64 MiB of HBM per device.

v0:
```python
import math
import jax
import jax.numpy as jnp
from jax import lax
from jax.sharding import PartitionSpec as P

NFFT = 512
NBLK = 7
HALF = 4
SHIFTS = 9
ORDER = SHIFTS * NBLK
ENTRIES = 2 * ORDER * ORDER


def transform_table(freqs, alpha):
    sample_index = jnp.arange(NFFT, dtype=jnp.int32)
    shift_index = jnp.arange(SHIFTS, dtype=jnp.int32) - HALF
    freq_bins = jnp.mod(freqs[:, None] + shift_index[None, :] * alpha[0], NFFT)
    phase_steps = jnp.mod(freq_bins[:, :, None] * sample_index[None, None, :], NFFT)
    phase = phase_steps.astype(jnp.float32) * (2.0 * math.pi / NFFT)
    sample_float = sample_index.astype(jnp.float32)
    window_shape = 0.5 - 0.5 * jnp.cos(sample_float * (2.0 * math.pi / NFFT))
    window_scale = window_shape / jnp.sqrt(jnp.sum(window_shape * window_shape))
    real_part = window_scale * jnp.cos(phase)
    imag_part = -(window_scale * jnp.sin(phase))
    return jnp.stack([real_part, imag_part], axis=1).astype(jnp.bfloat16)


def split_quadrants(products, order):
    real_gram = products[..., :order, :order] + products[..., order:, order:]
    imag_gram = products[..., :order, order:] - products[..., order:, :order]
    return jnp.stack([real_gram, imag_gram], axis=-3)


def per_device(series, starts, freqs, alpha):
    slab_cells = series.shape[1]
    n_space = lax.axis_size("space")
    n_freq = freqs.shape[0]
    total_cells = slab_cells * n_space
    cells = slab_cells // n_freq
    piece = -(-ENTRIES // (n_space * 128)) * 128
    rows = lax.all_to_all(series, "freq", split_axis=1, concat_axis=0, tiled=True)
    flat_table = transform_table(freqs, alpha).reshape(n_freq * 2 * SHIFTS, NFFT)
    blocks = []
    for block in range(NBLK):
        block_rows = lax.dynamic_slice_in_dim(rows, starts[block], NFFT, 0)
        spec_block = jnp.dot(flat_table, block_rows, preferred_element_type=jnp.float32)
        blocks.append(spec_block.astype(jnp.bfloat16).reshape(n_freq, 2, SHIFTS, cells))
    blockspec = jnp.stack(blocks, axis=3)
    stacked = blockspec.reshape(n_freq, 2 * ORDER, cells)
    products = jnp.einsum("jrc,jsc->jrs", stacked, stacked, preferred_element_type=jnp.float32)
    partial = split_quadrants(products, ORDER).reshape(n_freq, ENTRIES).astype(jnp.bfloat16)
    partial = jnp.pad(partial, ((0, 0), (0, n_space * piece - ENTRIES)))
    partial = jnp.transpose(partial.reshape(n_freq, n_space, piece), (1, 0, 2))
    gathered = lax.all_to_all(partial, "space", split_axis=0, concat_axis=0, tiled=True)
    slab_sum = jnp.sum(gathered.astype(jnp.float32), axis=0).astype(jnp.bfloat16)
    own = blockspec[:, :, HALF].reshape(n_freq, 2 * NBLK * cells)
    packed = jnp.concatenate([own, slab_sum], axis=1)
    packed = packed.reshape(n_freq, packed.shape[1] // 128, 128)
    received = lax.all_to_all(packed, "freq", split_axis=0, concat_axis=0, tiled=True)
    received = received.reshape(n_freq, -1)
    own = received[:, : 2 * NBLK * cells].reshape(n_freq, 2, NBLK, cells)
    spectra = jnp.transpose(own, (1, 2, 0, 3)).reshape(1, 2, NBLK, slab_cells)
    gram_piece = jnp.sum(received[:, 2 * NBLK * cells :].astype(jnp.float32), axis=0)
    spread = jnp.broadcast_to(
        gram_piece.reshape(1, piece // 128, 128), (n_space, piece // 128, 128)
    )
    pieces = lax.all_to_all(spread, "space", split_axis=0, concat_axis=0, tiled=True)
    gram = pieces.reshape(-1)[:ENTRIES].reshape(1, 2, ORDER, ORDER) / total_cells
    return (spectra, gram)


def solution(mesh):
    placed = (P("freq", "space"), P(), P(), P())
    return jax.shard_map(
        per_device,
        mesh=mesh,
        in_specs=placed,
        out_specs=(P("freq", None, None, "space"), P("freq", None, None, None)),
        check_vma=False,
    )
```

profile of v0, /device:TPU:4, one launch (start us, length us, event | category | flops | bytes accessed | tf_op | source)
XLA Modules:
  0.0 204.1 jit_solution(17525329280515386806)
XLA Ops:
  0.6 2.3 %copy.49 = bf16[4,64,8,256]{3,2,0,1:T(8,128)(2,1)} copy(bf16[4,64,8,256]{3,2,1,0:T(8,128)(2,1)} %bitcast.54) | data formatting | bytes 2097152 | tf_op jit(solution)/shard_map/all_to_all | solution.py:42
  3.0 18.9 %all-to-all-start = ((bf16[32,64,256]{2,0,1:T(8,128)(2,1)}), bf16[32,64,256]{2,0,1:T(8,128)(2,1)}, u32[]{:S(2)}, u32[]{:S(2)}) async-start(bf16[32,64,256]{2,0,1:T(8,128)(2,1)} %bitcast.45), calls=%async_computation | async-start | bytes 2097152 | tf_op jit(solution)/shard_map/all_to_all | solution.py:42
  21.9 0.7 fusion.28
  31.8 0.6 multiply_reduce_fusion
  33.3 5.4 %multiply_convert_fusion = (bf16[64,1,9,512]{3,0,2,1:T(8,128)(2,1)S(1)}, bf16[64,1,9,512]{3,0,2,1:T(8,128)(2,1)S(1)}) fusion(s32[64,9]{0,1:T(8,128)S(1)} %add_select_fusion.2, f32[512]{0:T(512)S(1)} %fusion.20), kind=kLoop, calls=%fused_computation.22 | loop fusion | flops 5603328 | bytes 1184000 | tf_op jit(solution)/shard_map/convert.5
  38.8 0.8 copy.30
  39.6 0.6 convert_element_type.62
  44.5 33.4 %all-to-all-done = bf16[32,64,256]{2,0,1:T(8,128)(2,1)} async-done(((bf16[32,64,256]{2,0,1:T(8,128)(2,1)}), bf16[32,64,256]{2,0,1:T(8,128)(2,1)}, u32[]{:S(2)}, u32[]{:S(2)}) %all-to-all-start) | async-done | bytes 1048608 | tf_op jit(solution)/shard_map/all_to_all | solution.py:42
  77.9 1.5 convolution_convert_fusion.6
  79.6 1.0 constant_dynamic-update-slice_fusion.6
  80.6 1.5 convolution_convert_fusion.5
  82.3 2.3 %convolution_convert_fusion.4 = bf16[1152,256]{1,0:T(8,128)(2,1)} fusion(bf16[1152,512]{1,0:T(8,128)(2,1)S(1)} %convert_element_type.62, bf16[2048,256]{1,0:T(8,128)(2,1)} %bitcast.2, s32[]{:T(128)S(6)} %select_n.53), kind=kOutput, calls=%fused_computation.6 | convolution fusion | flops 302284800 | bytes 2031620 | tf_op jit(solution)/shard_map/dot_general | solution.py:47
  84.7 1.3 stack_reshape.23
  86.0 2.3 %convolution_convert_fusion.3 = bf16[1152,256]{1,0:T(8,128)(2,1)} fusion(bf16[1152,512]{1,0:T(8,128)(2,1)S(1)} %convert_element_type.62, bf16[2048,256]{1,0:T(8,128)(2,1)} %bitcast.2, s32[]{:T(128)S(6)} %select_n.54), kind=kOutput, calls=%fused_computation.5 | convolution fusion | flops 302284800 | bytes 2031620 | tf_op jit(solution)/shard_map/dot_general | solution.py:47
  88.3 2.2 %stack_reshape.24 = bf16[64,2,9,1,256]{4,2,1,0,3:T(8,128)(2,1)} reshape(bf16[1152,256]{1,0:T(8,128)(2,1)} %convolution_convert_fusion.3) | data formatting | bytes 1179648 | tf_op jit(solution)/shard_map/stack;reshape | solution.py:49
  90.5 2.3 %convolution_convert_fusion.2 = bf16[1152,256]{1,0:T(8,128)(2,1)} fusion(bf16[1152,512]{1,0:T(8,128)(2,1)S(1)} %convert_element_type.62, bf16[2048,256]{1,0:T(8,128)(2,1)} %bitcast.2, s32[]{:T(128)S(6)} %select_n.55), kind=kOutput, calls=%fused_computation.4 | convolution fusion | flops 302284800 | bytes 2031620 | tf_op jit(solution)/shard_map/dot_general | solution.py:47
  92.8 2.1 %stack_reshape.25 = bf16[64,2,9,1,256]{4,2,1,0,3:T(8,128)(2,1)} reshape(bf16[1152,256]{1,0:T(8,128)(2,1)} %convolution_convert_fusion.2) | data formatting | bytes 1179648 | tf_op jit(solution)/shard_map/stack;reshape | solution.py:49
  94.9 2.3 %convolution_convert_fusion.1 = bf16[1152,256]{1,0:T(8,128)(2,1)} fusion(bf16[1152,512]{1,0:T(8,128)(2,1)S(1)} %convert_element_type.62, bf16[2048,256]{1,0:T(8,128)(2,1)} %bitcast.2, s32[]{:T(128)S(6)} %select_n.56), kind=kOutput, calls=%fused_computation.3 | convolution fusion | flops 302284800 | bytes 2031620 | tf_op jit(solution)/shard_map/dot_general | solution.py:47
  97.2 2.1 %stack_reshape.26 = bf16[64,2,9,1,256]{4,2,1,0,3:T(8,128)(2,1)} reshape(bf16[1152,256]{1,0:T(8,128)(2,1)} %convolution_convert_fusion.1) | data formatting | bytes 1179648 | tf_op jit(solution)/shard_map/stack;reshape | solution.py:49
  99.3 2.3 %convolution_convert_fusion = bf16[1152,256]{1,0:T(8,128)(2,1)} fusion(bf16[1152,512]{1,0:T(8,128)(2,1)S(1)} %convert_element_type.62, bf16[2048,256]{1,0:T(8,128)(2,1)} %bitcast.2, s32[]{:T(128)S(6)} %select_n.57), kind=kOutput, calls=%fused_computation.2 | convolution fusion | flops 302284800 | bytes 2031620 | tf_op jit(solution)/shard_map/dot_general | solution.py:47
  101.6 1.5 stack_reshape.27
  103.1 1.1 constant_dynamic-update-slice_fusion.5
  104.2 1.1 constant_dynamic-update-slice_fusion.4
  105.2 0.5 copy-done
  105.8 1.0 constant_dynamic-update-slice_fusion.3
  106.8 0.6 copy-done.1
  107.4 1.0 constant_dynamic-update-slice_fusion.2
  108.4 0.6 copy-done.2
  109.0 1.1 constant_dynamic-update-slice_fusion.1
  110.0 1.1 constant_dynamic-update-slice_fusion
  111.1 5.6 %copy.33 = bf16[64,2,9,7,256]{4,0,3,2,1:T(8,128)(2,1)S(1)} copy(bf16[64,2,9,7,256]{4,2,1,0,3:T(8,128)(2,1)} %constant_dynamic-update-slice_fusion) | data formatting | bytes 8257536 | tf_op jit(solution)/shard_map/stack | solution.py:49
  116.7 4.6 %fusion = f32[64,126,126]{2,1,0:T(8,128)S(1)} fusion(bf16[64,126,256]{2,0,1:T(8,128)(2,1)S(1)} %bitcast.48), kind=kOutput, calls=%fused_computation | convolution fusion | flops 520224768 | bytes 8193024 | tf_op jit(solution)/shard_map/jrc,jsc->jrs/dot_general | solution.py:51
  121.4 1.2 fusion.10
  122.6 0.5 pad_maximum_fusion
  123.2 3.3 %convert_element_type.70 = bf16[64,7938]{1,0:T(8,128)(2,1)S(1)} reshape(bf16[64,2,63,63]{3,2,1,0:T(8,128)(2,1)S(1)} %copy.36) | data formatting | bytes 2032128 | tf_op jit(solution)/shard_map/convert_element_type | solution.py:52
  126.6 1.1 copy.48
  127.7 5.1 %all-to-all-start.1 = ((bf16[8,64,1024]{2,1,0:T(8,128)(2,1)}), bf16[8,64,1024]{2,1,0:T(8,128)(2,1)S(1)}, u32[]{:S(2)}, u32[]{:S(2)}) async-start(bf16[8,64,1024]{2,1,0:T(8,128)(2,1)} %bitcast.44), calls=%async_computation.1 | async-start | bytes 2097152 | tf_op jit(solution)/shard_map/all_to_all | solution.py:55
  132.8 3.0 %slice.60 = bf16[64,2,1,7,256]{4,2,1,0,3:T(2,128)(2,1)S(1)} slice(bf16[64,2,9,7,256]{4,2,1,0,3:T(8,128)(2,1)} %constant_dynamic-update-slice_fusion), slice={[0:64], [0:2], [4:5], [0:7], [0:256]} | slice | bytes 917504 | tf_op jit(solution)/shard_map/slice | solution.py:57
  135.8 0.5 copy.32
  136.3 0.5 reshape_squeeze.3
  136.8 9.9 %all-to-all-done.1 = bf16[8,64,1024]{2,1,0:T(8,128)(2,1)S(1)} async-done(((bf16[8,64,1024]{2,1,0:T(8,128)(2,1)}), bf16[8,64,1024]{2,1,0:T(8,128)(2,1)S(1)}, u32[]{:S(2)}, u32[]{:S(2)}) %all-to-all-start.1) | async-done | bytes 1048608 | tf_op jit(solution)/shard_map/all_to_all | solution.py:55
  147.3 45.3 %all_to_all.34 = bf16[64,36,128]{2,1,0:T(8,128)(2,1)S(1)} all-to-all(bf16[64,36,128]{2,1,0:T(8,128)(2,1)S(1)} %reshape.166), channel_id=1, replica_groups=mesh['freq'=64,'space'=8] {'freq'}, dimensions={0} | all-to-all | bytes 1179648 | tf_op jit(solution)/shard_map/all_to_all | solution.py:60
  192.7 0.6 broadcast_in_dim.5
  193.3 3.6 %all-to-all-start.3 = ((f32[8,8,128]{2,1,0:T(8,128)}), f32[8,8,128]{2,1,0:T(8,128)S(1)}, u32[]{:S(2)}, u32[]{:S(2)}) async-start(f32[8,8,128]{2,1,0:T(8,128)} %broadcast_in_dim.5), calls=%async_computation.3 | async-start | bytes 65536 | tf_op jit(solution)/shard_map/all_to_all | solution.py:68
  197.0 0.5 reshape.168
  197.7 0.9 reshape.169
  198.6 4.6 %all-to-all-done.3 = f32[8,8,128]{2,1,0:T(8,128)S(1)} async-done(((f32[8,8,128]{2,1,0:T(8,128)}), f32[8,8,128]{2,1,0:T(8,128)S(1)}, u32[]{:S(2)}, u32[]{:S(2)}) %all-to-all-start.3) | async-done | bytes 32800 | tf_op jit(solution)/shard_map/all_to_all | solution.py:68
  203.4 0.7 copy.39
  (24 shorter events, 2.0 us)
Async XLA Ops:
  3.0 18.9 %copy-start.3 = (s32[7]{0:T(128)S(1)}, s32[7]{0:T(128)}, u32[]{:S(2)}) copy-start(s32[7]{0:T(128)} %param.5) | copy-start | bytes 88
  3.0 30.3 %copy-start.4 = (s32[64]{0:T(128)S(1)}, s32[64]{0:T(128)}, u32[]{:S(2)}) copy-start(s32[64]{0:T(128)} %param.6) | copy-start | bytes 772
  3.0 74.9 %all-to-all-start = ((bf16[32,64,256]{2,0,1:T(8,128)(2,1)}), bf16[32,64,256]{2,0,1:T(8,128)(2,1)}, u32[]{:S(2)}, u32[]{:S(2)}) async-start(bf16[32,64,256]{2,0,1:T(8,128)(2,1)} %bitcast.45), calls=%async_computation | async-start | bytes 2097152 | tf_op jit(solution)/shard_map/all_to_all | solution.py:42
  104.2 1.6 copy-start
  105.8 1.6 copy-start.1
  107.4 1.6 copy-start.2
  127.7 19.0 %all-to-all-start.1 = ((bf16[8,64,1024]{2,1,0:T(8,128)(2,1)}), bf16[8,64,1024]{2,1,0:T(8,128)(2,1)S(1)}, u32[]{:S(2)}, u32[]{:S(2)}) async-start(bf16[8,64,1024]{2,1,0:T(8,128)(2,1)} %bitcast.44), calls=%async_computation.1 | async-start | bytes 2097152 | tf_op jit(solution)/shard_map/all_to_all | solution.py:55
  193.3 9.9 %all-to-all-start.3 = ((f32[8,8,128]{2,1,0:T(8,128)}), f32[8,8,128]{2,1,0:T(8,128)S(1)}, u32[]{:S(2)}, u32[]{:S(2)}) async-start(f32[8,8,128]{2,1,0:T(8,128)} %broadcast_in_dim.5), calls=%async_computation.3 | async-start | bytes 65536 | tf_op jit(solution)/shard_map/all_to_all | solution.py:68
where the time goes:
time: 205 us; the launch traced here: 204 us
  waiting for transfers between devices  48 us (23%)
  blocking collectives  45.3 us (22%)
  local copies, waits for them, and re-layouts  40.9 us (20%)
  starting transfers between devices  27.7 us (14%)
  matrix products  19 us (9%)
  between operations  15.1 us (7%)
  other arithmetic  8.18 us (4%)
    all_to_all x1, blocking collectives, per_device(): lax.all_to_all(packed, 'freq', split_axis=0, concat_axis=0, tiled=True)  45.3 us
    all_to_all x1, waiting for transfers between devices, per_device(): lax.all_to_all(series, 'freq', split_axis=1, concat_axis=0, tiled=True)  33.4 us
    all_to_all x1, starting transfers between devices, per_device(): lax.all_to_all(series, 'freq', split_axis=1, concat_axis=0, tiled=True)  18.9 us
    another operation x9, local copies, waits for them, and re-layouts, per_device(): blockspec = jnp.stack(blocks, axis=3)  16.4 us
    dot_general x7, matrix products, per_device(): jnp.dot(flat_table, block_rows, preferred_element_type=jnp.float32)  14.3 us
    all_to_all x1, waiting for transfers between devices, per_device(): lax.all_to_all(partial, 'space', split_axis=0, concat_axis=0, tiled=True)  9.93 us
    unnamed x18, local copies, waits for them, and re-layouts  8.78 us
    another operation x1, other arithmetic  5.37 us
  transfers between devices with their start and end apart: 3, of which 3 were waited for; matrix products, arithmetic and copies ran while one was open for 7% of the time, Pallas kernels for 0%

commit v1 on v0

--- a/solution.py
+++ b/solution.py
@@ -39,7 +39,16 @@
     total_cells = slab_cells * n_space
     cells = slab_cells // n_freq
     piece = -(-ENTRIES // (n_space * 128)) * 128
-    rows = lax.all_to_all(series, "freq", split_axis=1, concat_axis=0, tiled=True)
+
+    def perform_region(chunk, along_dim, dim_i):
+        return jnp.concatenate(
+            lax.all_to_all(
+                jnp.stack(jnp.split(chunk, lax.axis_size("freq"), axis=along_dim)), "freq", 0, 0
+            ),
+            axis=dim_i,
+        )
+
+    rows = perform_region(series, 1, 0)
     flat_table = transform_table(freqs, alpha).reshape(n_freq * 2 * SHIFTS, NFFT)
     blocks = []
     for block in range(NBLK):

time: 205 us -> 291 us (1.42); the launches traced: 204 us -> 286 us
  local copies, waits for them, and re-layouts: 40.9 us -> 123 us
    unnamed x18 -> x81, local copies, waits for them, and re-layouts: 8.78 us -> 91.8 us
  transfers between devices with their start and end apart: 3 -> 3, of which waited for: 3 -> 3; matrix products, arithmetic and copies ran while one was open for 7% -> 5% of each run, Pallas kernels for 0% -> 0%
where the time goes in v1:
time: 291 us; the launch traced here: 286 us
  local copies, waits for them, and re-layouts  123 us (42%)
  waiting for transfers between devices  48 us (16%)
  blocking collectives  45.3 us (16%)
  starting transfers between devices  27.5 us (9%)
  matrix products  18.9 us (6%)
  between operations  15.1 us (5%)
  other arithmetic  8.18 us (3%)
    unnamed x81, local copies, waits for them, and re-layouts  91.8 us
    all_to_all x1, blocking collectives, per_device(): lax.all_to_all(packed, 'freq', split_axis=0, concat_axis=0, tiled=True)  45.3 us
    all_to_all x1, waiting for transfers between devices, perform_region(): lax.all_to_all(jnp.stack(jnp.split(chunk, lax.axis_size('freq'), axis=alo...  33.4 us
    all_to_all x1, starting transfers between devices, perform_region(): lax.all_to_all(jnp.stack(jnp.split(chunk, lax.axis_size('freq'), axis=alo...  18.8 us
    another operation x9, local copies, waits for them, and re-layouts, per_device(): blockspec = jnp.stack(blocks, axis=3)  16.4 us
    dot_general x7, matrix products, per_device(): jnp.dot(flat_table, block_rows, preferred_element_type=jnp.float32)  14.3 us
    all_to_all x1, waiting for transfers between devices, per_device(): lax.all_to_all(partial, 'space', split_axis=0, concat_axis=0, tiled=True)  9.92 us
  transfers between devices with their start and end apart: 3, of which 3 were waited for; matrix products, arithmetic and copies ran while one was open for 5% of the time, Pallas kernels for 0%

profile of v1, /device:TPU:4, one launch (start us, length us, event | category | flops | bytes accessed | tf_op | source)
XLA Modules:
  0.0 286.0 jit_solution(7362460236017686288)
XLA Ops:
  0.6 1.3 constant_dynamic-update-slice_fusion.63
  1.9 1.3 constant_dynamic-update-slice_fusion.62
  7.2 1.3 constant_dynamic-update-slice_fusion.58
  8.5 1.3 constant_dynamic-update-slice_fusion.57
  11.2 1.3 constant_dynamic-update-slice_fusion.55
  16.4 1.3 constant_dynamic-update-slice_fusion.51
  17.8 1.3 constant_dynamic-update-slice_fusion.50
  21.7 1.3 constant_dynamic-update-slice_fusion.47
  24.3 1.3 constant_dynamic-update-slice_fusion.45
  27.0 1.3 constant_dynamic-update-slice_fusion.43
  29.6 1.3 constant_dynamic-update-slice_fusion.41
  36.2 1.3 constant_dynamic-update-slice_fusion.36
  37.5 1.3 constant_dynamic-update-slice_fusion.35
  38.8 1.3 constant_dynamic-update-slice_fusion.34
  42.8 1.3 constant_dynamic-update-slice_fusion.31
  49.4 1.3 constant_dynamic-update-slice_fusion.26
  61.2 1.3 constant_dynamic-update-slice_fusion.17
  63.8 1.3 constant_dynamic-update-slice_fusion.15
  65.2 1.3 constant_dynamic-update-slice_fusion.14
  67.8 1.3 constant_dynamic-update-slice_fusion.12
  73.1 1.3 constant_dynamic-update-slice_fusion.8
  74.4 1.3 constant_dynamic-update-slice_fusion.7
  77.0 1.3 constant_dynamic-update-slice_fusion.5
  81.0 1.3 constant_dynamic-update-slice_fusion.2
  82.3 1.3 constant_dynamic-update-slice_fusion.1
  85.0 18.8 %all-to-all-start = ((bf16[64,32,256]{2,1,0:T(8,128)(2,1)}), bf16[64,32,256]{2,1,0:T(8,128)(2,1)}, u32[]{:S(2)}, u32[]{:S(2)}) async-start(bf16[64,32,256]{2,1,0:T(8,128)(2,1)} %constant_dynamic-update-slice_fusion), calls=%async_computation | async-start | bytes 2097152 | tf_op jit(solution)/shard_map/all_to_all | solution.py:45
  115.2 5.4 %multiply_convert_fusion = (bf16[64,1,9,512]{3,0,2,1:T(8,128)(2,1)S(1)}, bf16[64,1,9,512]{3,0,2,1:T(8,128)(2,1)S(1)}) fusion(s32[64,9]{0,1:T(8,128)S(1)} %add_select_fusion.2, f32[512]{0:T(512)S(1)} %fusion.20), kind=kLoop, calls=%fused_computation.22 | loop fusion | flops 5603328 | bytes 1184000 | tf_op jit(solution)/shard_map/convert.5
  126.3 33.4 %all-to-all-done = bf16[64,32,256]{2,1,0:T(8,128)(2,1)} async-done(((bf16[64,32,256]{2,1,0:T(8,128)(2,1)}), bf16[64,32,256]{2,1,0:T(8,128)(2,1)}, u32[]{:S(2)}, u32[]{:S(2)}) %all-to-all-start) | async-done | bytes 1048608 | tf_op jit(solution)/shard_map/all_to_all | solution.py:45
  159.8 1.4 convolution_convert_fusion.6
  162.5 1.4 convolution_convert_fusion.5
  164.2 2.3 convolution_convert_fusion.4
  167.8 2.3 convolution_convert_fusion.3
  170.1 2.2 stack_reshape.24
  172.3 2.3 convolution_convert_fusion.2
  174.6 2.1 stack_reshape.25
  176.7 2.3 convolution_convert_fusion.1
  179.0 2.1 stack_reshape.26
  181.2 2.3 convolution_convert_fusion
  183.4 1.5 stack_reshape.27
  192.9 5.6 %copy.30 = bf16[64,2,9,7,256]{4,0,3,2,1:T(8,128)(2,1)S(1)} copy(bf16[64,2,9,7,256]{4,2,1,0,3:T(8,128)(2,1)} %constant_dynamic-update-slice_fusion.64) | data formatting | bytes 8257536 | tf_op jit(solution)/shard_map/stack | solution.py:58
  198.6 4.6 %fusion = f32[64,126,126]{2,1,0:T(8,128)S(1)} fusion(bf16[64,126,256]{2,0,1:T(8,128)(2,1)S(1)} %bitcast.170), kind=kOutput, calls=%fused_computation | convolution fusion | flops 520224768 | bytes 8193024 | tf_op jit(solution)/shard_map/jrc,jsc->jrs/dot_general | solution.py:60
  205.1 3.3 %convert_element_type.70 = bf16[64,7938]{1,0:T(8,128)(2,1)S(1)} reshape(bf16[64,2,63,63]{3,2,1,0:T(8,128)(2,1)S(1)} %copy.33) | data formatting | bytes 2032128 | tf_op jit(solution)/shard_map/convert_element_type | solution.py:61
  209.5 5.1 %all-to-all-start.1 = ((bf16[8,64,1024]{2,1,0:T(8,128)(2,1)}), bf16[8,64,1024]{2,1,0:T(8,128)(2,1)S(1)}, u32[]{:S(2)}, u32[]{:S(2)}) async-start(bf16[8,64,1024]{2,1,0:T(8,128)(2,1)} %bitcast.167), calls=%async_computation.1 | async-start | bytes 2097152 | tf_op jit(solution)/shard_map/all_to_all | solution.py:64
  214.6 3.0 %slice.60 = bf16[64,2,1,7,256]{4,2,1,0,3:T(2,128)(2,1)S(1)} slice(bf16[64,2,9,7,256]{4,2,1,0,3:T(8,128)(2,1)} %constant_dynamic-update-slice_fusion.64), slice={[0:64], [0:2], [4:5], [0:7], [0:256]} | slice | bytes 917504 | tf_op jit(solution)/shard_map/slice | solution.py:66
  218.6 9.9 %all-to-all-done.1 = bf16[8,64,1024]{2,1,0:T(8,128)(2,1)S(1)} async-done(((bf16[8,64,1024]{2,1,0:T(8,128)(2,1)}), bf16[8,64,1024]{2,1,0:T(8,128)(2,1)S(1)}, u32[]{:S(2)}, u32[]{:S(2)}) %all-to-all-start.1) | async-done | bytes 1048608 | tf_op jit(solution)/shard_map/all_to_all | solution.py:64
  229.1 45.3 %all_to_all.20 = bf16[64,36,128]{2,1,0:T(8,128)(2,1)S(1)} all-to-all(bf16[64,36,128]{2,1,0:T(8,128)(2,1)S(1)} %reshape.167), channel_id=1, replica_groups=mesh['freq'=64,'space'=8] {'freq'}, dimensions={0} | all-to-all | bytes 1179648 | tf_op jit(solution)/shard_map/all_to_all | solution.py:69
  275.2 3.6 %all-to-all-start.3 = ((f32[8,8,128]{2,1,0:T(8,128)}), f32[8,8,128]{2,1,0:T(8,128)S(1)}, u32[]{:S(2)}, u32[]{:S(2)}) async-start(f32[8,8,128]{2,1,0:T(8,128)} %broadcast_in_dim.5), calls=%async_computation.3 | async-start | bytes 65536 | tf_op jit(solution)/shard_map/all_to_all | solution.py:77
  280.4 4.6 %all-to-all-done.3 = f32[8,8,128]{2,1,0:T(8,128)S(1)} async-done(((f32[8,8,128]{2,1,0:T(8,128)}), f32[8,8,128]{2,1,0:T(8,128)S(1)}, u32[]{:S(2)}, u32[]{:S(2)}) %all-to-all-start.3) | async-done | bytes 32800 | tf_op jit(solution)/shard_map/all_to_all | solution.py:77
  (87 shorter events, 72.7 us)
Async XLA Ops:
  74.4 29.4 %copy-start.3 = (s32[7]{0:T(128)S(1)}, s32[7]{0:T(128)}, u32[]{:S(2)}) copy-start(s32[7]{0:T(128)} %param.5) | copy-start | bytes 88
  77.0 38.1 %copy-start.4 = (s32[64]{0:T(128)S(1)}, s32[64]{0:T(128)}, u32[]{:S(2)}) copy-start(s32[64]{0:T(128)} %param.6) | copy-start | bytes 772
  85.0 74.8 %all-to-all-start = ((bf16[64,32,256]{2,1,0:T(8,128)(2,1)}), bf16[64,32,256]{2,1,0:T(8,128)(2,1)}, u32[]{:S(2)}, u32[]{:S(2)}) async-start(bf16[64,32,256]{2,1,0:T(8,128)(2,1)} %constant_dynamic-update-slice_fusion), calls=%async_computation | async-start | bytes 2097152 | tf_op jit(solution)/shard_map/all_to_all | solution.py:45
  186.0 1.6 copy-start
  187.6 1.6 copy-start.1
  189.2 1.6 copy-start.2
  209.5 19.0 %all-to-all-start.1 = ((bf16[8,64,1024]{2,1,0:T(8,128)(2,1)}), bf16[8,64,1024]{2,1,0:T(8,128)(2,1)S(1)}, u32[]{:S(2)}, u32[]{:S(2)}) async-start(bf16[8,64,1024]{2,1,0:T(8,128)(2,1)} %bitcast.167), calls=%async_computation.1 | async-start | bytes 2097152 | tf_op jit(solution)/shard_map/all_to_all | solution.py:64
  275.2 9.9 %all-to-all-start.3 = ((f32[8,8,128]{2,1,0:T(8,128)}), f32[8,8,128]{2,1,0:T(8,128)S(1)}, u32[]{:S(2)}, u32[]{:S(2)}) async-start(f32[8,8,128]{2,1,0:T(8,128)} %broadcast_in_dim.5), calls=%async_computation.3 | async-start | bytes 65536 | tf_op jit(solution)/shard_map/all_to_all | solution.py:77
